TPU v7x, 128 devices: a whole 4x4x4 slice. The times are simulated.
128 devices in a mesh: edata: 8 (over y, x_hi), tensor: 16 (over z, x_lo, core).
Axes of the slice: x: 4 (x_hi: 2, x_lo: 2; x = x_hi * 2 + x_lo), y: 4, z: 4, core: 2. Of those that a mesh axis runs over, the one named last changes fastest.
Arguments:
- tokens: bfloat16 [2048, 6144], P('tensor', 'edata'), may hold values from -6 to 6
- expert_ids: int32 [2048, 2], P('tensor'), may hold values from 0 to 7, as said below
- route_weight: float32 [2048, 2], P('tensor'), may hold values from 0.25 to 1
- up_weight: bfloat16 [2, 6144, 16384], P(None, 'edata', 'tensor'), may hold values from -0.078125 to 0.078125
- down_weight: bfloat16 [2, 16384, 6144], P(None, 'tensor', 'edata'), may hold values from -0.046875 to 0.046875
- target_up: bfloat16 [2, 6144, 16384], P(None, 'edata', 'tensor'), may hold values from -0.078125 to 0.078125
- target_down: bfloat16 [2, 16384, 6144], P(None, 'tensor', 'edata'), may hold values from -0.046875 to 0.046875
- cotangent: bfloat16 [2048, 6144], P('tensor', 'edata'), may hold values from -6 to 6
Outputs:
- mixed: bfloat16 [2048, 6144], P('tensor', 'edata')
- grad_tokens: bfloat16 [2048, 6144], P('tensor', 'edata')
- grad_up: bfloat16 [2, 6144, 16384], P(None, 'edata', 'tensor')
- grad_down: bfloat16 [2, 16384, 6144], P(None, 'tensor', 'edata')
- target_mixed: bfloat16 [2048, 6144], P('tensor', 'edata')
Inputs may be any that keep to these rules, and one draw needn't show every extreme that they name: `expert_ids`: every token names 2 different experts. Among the 128 tokens of one tensor index no expert is named by more than 48 tokens, and expert 0 is named by exactly 48.
All inputs are finite; a program needn't handle non-finite values.
Results may differ from a plain program's by a relative error of at most 0.03.
Values may be sent and summed in bfloat16 or wider, within the bound.
No kernel may reach another device: no remote copies, remote signals or barrier semaphores. Data moves between devices by JAX's collectives and lax.ppermute only.
A program may use at most 128 MiB of HBM per device.

v0:
```python
import jax
import jax.numpy as jnp
from jax import lax
from jax.sharding import PartitionSpec as P

EXP_WIN = 2
CAP = 48


def tables(expert_ids, route_weight):
    placed_list, portion_list = ([], [])
    for expert in range(EXP_WIN):
        chosen = expert_ids == expert
        listed = jnp.any(chosen, axis=1)
        position = jnp.cumsum(listed.astype(jnp.int32)) - 1
        placed = (position[None, :] == jnp.arange(CAP, dtype=jnp.int32)[:, None]) & listed[None, :]
        weight = jnp.sum(jnp.where(chosen, route_weight, 0.0), axis=1)
        placed_list.append(placed)
        portion_list.append(jnp.where(placed, weight[None, :], 0.0))
    onehot = jnp.stack(placed_list, axis=1).astype(jnp.bfloat16)
    combine = jnp.stack(portion_list, axis=1)
    return (onehot, combine)


def combined(owner_out, combine):
    return jnp.einsum("ced,cet->td", owner_out, combine, precision=lax.Precision.HIGHEST).astype(
        jnp.bfloat16
    )


def silu_round(summed):
    return jax.nn.silu(summed).astype(jnp.bfloat16)


def shards(
    tokens, expert_ids, route_weight, up_weight, down_weight, target_up, target_down, cotangent
):
    onehot, combine = tables(expert_ids, route_weight)
    picked = jnp.einsum("cet,td->ced", onehot, tokens, preferred_element_type=jnp.float32).astype(
        jnp.bfloat16
    )
    scaled = jnp.einsum(
        "cet,td->ced", combine, cotangent.astype(jnp.float32), precision=lax.Precision.HIGHEST
    ).astype(jnp.bfloat16)
    gathered_x, gathered_g = (
        lax.all_gather(picked, "tensor", axis=0, tiled=True),
        lax.all_gather(scaled, "tensor", axis=0, tiled=True),
    )
    routed = gathered_x.shape[0]
    share_rows = routed // lax.axis_size("edata")
    owner_rows = routed // lax.axis_size("tensor")

    def edata_sum(term_fn, act_fn):
        summed = lax.psum_scatter(
            term_fn(jnp.int32(0), share_rows * lax.axis_size("edata")).astype(jnp.bfloat16),
            "edata",
            scatter_dimension=0,
            tiled=True,
        ).astype(jnp.float32)
        acted = lax.all_gather(act_fn(summed), "edata", axis=0, tiled=True)
        return (acted, summed)

    def tensor_sum(term_fn):
        return lax.psum_scatter(
            term_fn(jnp.int32(0), owner_rows * lax.axis_size("tensor")).astype(jnp.bfloat16),
            "tensor",
            scatter_dimension=0,
            tiled=True,
        ).astype(jnp.float32)

    def up_term(source, weight):

        def partial_up(begin_row, row_count):
            return jnp.einsum("red,edf->ref", source, weight, preferred_element_type=jnp.float32)

        return partial_up

    def down_term(source, weight):

        def partial_down(begin_row, row_count):
            return jnp.einsum("ref,efd->red", source, weight, preferred_element_type=jnp.float32)

        return partial_down

    def back_term(begin_row, row_count):
        return jnp.einsum(
            "red,efd->ref", gathered_g, down_weight, preferred_element_type=jnp.float32
        )

    blend_up = (0.75 * target_up.astype(jnp.float32) + 0.25 * up_weight.astype(jnp.float32)).astype(
        jnp.bfloat16
    )
    blend_down = (
        0.75 * target_down.astype(jnp.float32) + 0.25 * down_weight.astype(jnp.float32)
    ).astype(jnp.bfloat16)
    active, hidden_pre = edata_sum(up_term(gathered_x, up_weight), silu_round)
    owner_out = tensor_sum(down_term(active, down_weight))
    mixed = combined(owner_out, combine)
    grad_down = jnp.einsum(
        "ref,red->efd", active, gathered_g, preferred_element_type=jnp.float32
    ).astype(jnp.bfloat16)

    def grad_act(summed):
        logistic = jax.nn.sigmoid(hidden_pre)
        return (summed * logistic * (1.0 + hidden_pre * (1.0 - logistic))).astype(jnp.bfloat16)

    grad_pre, unused = edata_sum(back_term, grad_act)
    grad_up = jnp.einsum(
        "red,ref->edf", gathered_x, grad_pre, preferred_element_type=jnp.float32
    ).astype(jnp.bfloat16)

    def grad_term(begin_row, row_count):
        return jnp.einsum("ref,edf->red", grad_pre, up_weight, preferred_element_type=jnp.float32)

    grad_rows = tensor_sum(grad_term)
    grad_tokens = combined(grad_rows, combine)
    target_active, unused_pre = edata_sum(up_term(gathered_x, blend_up), silu_round)
    target_out = tensor_sum(down_term(target_active, blend_down))
    target_mixed = combined(target_out, combine)
    return (mixed, grad_tokens, grad_up, grad_down, target_mixed)


def solution(mesh):
    return jax.shard_map(
        shards,
        mesh=mesh,
        in_specs=(
            P("tensor", "edata"),
            P("tensor", None),
            P("tensor", None),
            P(None, "edata", "tensor"),
            P(None, "tensor", "edata"),
            P(None, "edata", "tensor"),
            P(None, "tensor", "edata"),
            P("tensor", "edata"),
        ),
        out_specs=(
            P("tensor", "edata"),
            P("tensor", "edata"),
            P(None, "edata", "tensor"),
            P(None, "tensor", "edata"),
            P("tensor", "edata"),
        ),
        check_vma=False,
    )
```

profile of v0, /device:TPU:4, one launch (start us, length us, event | category | flops | bytes accessed | tf_op | source)
XLA Modules:
  0.0 728.4 jit_solution(15373005583422794436)
XLA Ops:
  12.4 34.4 %all-gather.6.cloned.1.call-done = bf16[768,2,768]{2,0,1:T(8,128)(2,1)} async-done(((bf16[48,2,768]{2,0,1:T(8,128)(2,1)}), bf16[768,2,768]{2,0,1:T(8,128)(2,1)}) %all-gather.6.cloned.1.call-update) | async-done | bytes 2359312 | tf_op jit(solution)/shard_map/all_gather | solution.py:46
  46.8 7.9 %convert_bitcast_fusion = bf16[768,2,1024]{2,0,1:T(8,128)(2,1)} fusion(bf16[768,2,768]{2,0,1:T(8,128)(2,1)} %all-gather.6.cloned.1.call-done, bf16[2,768,1024]{2,1,0:T(8,128)(2,1)} %param.11, bf16[2,768,1024]{2,1,0:T(8,128)(2,1)} %param.13), kind=kOutput, calls=%fused_computation.4 | convolution fusion | flops 2426929152 | bytes 11796480 | tf_op jit(solution)/shard_map/red,edf->ref/dot_general | solution.py:74
  54.8 28.7 %all-gather.10.cloned.1.call-done = bf16[768,2,768]{2,0,1:T(8,128)(2,1)} async-done(((bf16[48,2,768]{2,0,1:T(8,128)(2,1)}), bf16[768,2,768]{2,0,1:T(8,128)(2,1)}) %all-gather.10.cloned.1.call-update) | async-done | bytes 2359312 | tf_op jit(solution)/shard_map/all_gather | solution.py:47
  83.5 5.7 convert_bitcast_fusion.1
  91.1 5.6 convert_bitcast_fusion.2
  96.7 67.7 %reduce-scatter.15.cloned.1.call-done = bf16[96,2,1024]{2,0,1:T(8,128)(2,1)} async-done(((bf16[768,2,1024]{2,0,1:T(8,128)(2,1)}), bf16[96,2,1024]{2,0,1:T(8,128)(2,1)}) %reduce-scatter.15.cloned.1.call-update) | async-done | bytes 393232 | tf_op jit(solution)/shard_map/reduce_scatter | solution.py:54
  164.4 2.0 fusion.12
  166.5 80.2 %reduce-scatter.11.cloned.1.call-done = bf16[96,2,1024]{2,0,1:T(8,128)(2,1)} async-done(((bf16[768,2,1024]{2,0,1:T(8,128)(2,1)}), bf16[96,2,1024]{2,0,1:T(8,128)(2,1)}) %reduce-scatter.11.cloned.1.call-update) | async-done | bytes 393232 | tf_op jit(solution)/shard_map/reduce_scatter | solution.py:54
  246.7 82.3 %reduce-scatter.7.cloned.1.call-done = bf16[96,2,1024]{2,0,1:T(8,128)(2,1)} async-done(((bf16[768,2,1024]{2,0,1:T(8,128)(2,1)}), bf16[96,2,1024]{2,0,1:T(8,128)(2,1)}) %reduce-scatter.7.cloned.1.call-update) | async-done | bytes 393232 | tf_op jit(solution)/shard_map/reduce_scatter | solution.py:54
  329.0 2.4 fusion.19
  332.2 60.3 %all-gather.14.cloned.1.call-done = bf16[768,2,1024]{2,0,1:T(8,128)(2,1)} async-done(((bf16[96,2,1024]{2,0,1:T(8,128)(2,1)}), bf16[768,2,1024]{2,0,1:T(8,128)(2,1)}) %all-gather.14.cloned.1.call-update) | async-done | bytes 3145744 | tf_op jit(solution)/shard_map/all_gather | solution.py:60
  392.5 7.0 convert_bitcast_fusion.3
  399.6 56.3 %all-gather.8.cloned.1.call-done = bf16[768,2,1024]{2,0,1:T(8,128)(2,1)} async-done(((bf16[96,2,1024]{2,0,1:T(8,128)(2,1)}), bf16[768,2,1024]{2,0,1:T(8,128)(2,1)}) %all-gather.8.cloned.1.call-update) | async-done | bytes 3145744 | tf_op jit(solution)/shard_map/all_gather | solution.py:60
  455.9 6.8 convert_bitcast_fusion.5
  463.0 56.3 %all-gather.12.cloned.1.call-done = bf16[768,2,1024]{2,0,1:T(8,128)(2,1)} async-done(((bf16[96,2,1024]{2,0,1:T(8,128)(2,1)}), bf16[768,2,1024]{2,0,1:T(8,128)(2,1)}) %all-gather.12.cloned.1.call-update) | async-done | bytes 3145744 | tf_op jit(solution)/shard_map/all_gather | solution.py:60
  519.3 5.9 convert_bitcast_fusion.4
  525.3 7.1 convolution_convert_fusion
  532.4 4.1 convolution_convert_fusion.1
  536.4 50.9 %reduce-scatter.17.cloned.1.call-done = bf16[48,2,768]{2,0,1:T(8,128)(2,1)} async-done(((bf16[768,2,768]{2,0,1:T(8,128)(2,1)}), bf16[48,2,768]{2,0,1:T(8,128)(2,1)}) %reduce-scatter.17.cloned.1.call-update) | async-done | bytes 147472 | tf_op jit(solution)/shard_map/reduce_scatter | solution.py:64
  587.3 2.0 fusion.8
  589.3 64.3 %reduce-scatter.9.cloned.1.call-done = bf16[48,2,768]{2,0,1:T(8,128)(2,1)} async-done(((bf16[768,2,768]{2,0,1:T(8,128)(2,1)}), bf16[48,2,768]{2,0,1:T(8,128)(2,1)}) %reduce-scatter.9.cloned.1.call-update) | async-done | bytes 147472 | tf_op jit(solution)/shard_map/reduce_scatter | solution.py:64
  653.6 2.0 fusion.6
  655.5 64.4 %reduce-scatter.13.cloned.1.call-done = bf16[48,2,768]{2,0,1:T(8,128)(2,1)} async-done(((bf16[768,2,768]{2,0,1:T(8,128)(2,1)}), bf16[48,2,768]{2,0,1:T(8,128)(2,1)}) %reduce-scatter.13.cloned.1.call-update) | async-done | bytes 147472 | tf_op jit(solution)/shard_map/reduce_scatter | solution.py:64
  719.9 2.0 fusion.7
  (50 shorter events, 8.3 us)
Async XLA Ops:
  7.2 1.6 copy-start
  7.2 39.6 %all-gather.6.cloned.1.call-start = ((), (), s32[]{:S(2)}) async-start(), calls=%async_computation.6 | async-start | bytes 2506752 | tf_op jit(solution)/shard_map/all_gather | solution.py:46
  9.7 73.8 %all-gather.10.cloned.1.call-start = ((), (), s32[]{:S(2)}) async-start(), calls=%async_computation.10 | async-start | bytes 2506752 | tf_op jit(solution)/shard_map/all_gather | solution.py:47
  12.4 152.1 %reduce-scatter.15.cloned.1.call-start = ((), (), s32[]{:S(2)}) async-start(), calls=%async_computation.14 | async-start | bytes 3538944 | tf_op jit(solution)/shard_map/reduce_scatter | solution.py:54
  54.7 28.8 %copy-start.2 = (bf16[2,1024,768]{2,1,0:T(8,128)(2,1)S(1)}, bf16[2,1024,768]{2,1,0:T(8,128)(2,1)}, u32[]{:S(2)}) copy-start(bf16[2,1024,768]{2,1,0:T(8,128)(2,1)} %param.12) | copy-start | bytes 9437188
  54.7 192.0 %reduce-scatter.11.cloned.1.call-start = ((), (), s32[]{:S(2)}) async-start(), calls=%async_computation.11 | async-start | bytes 3538944 | tf_op jit(solution)/shard_map/reduce_scatter | solution.py:54
  89.2 1.9 copy-start.3
  89.2 239.8 %reduce-scatter.7.cloned.1.call-start = ((), (), s32[]{:S(2)}) async-start(), calls=%async_computation.7 | async-start | bytes 3538944 | tf_op jit(solution)/shard_map/reduce_scatter | solution.py:54
  96.7 295.8 %copy-start.1 = (bf16[2,1024,768]{2,1,0:T(8,128)(2,1)S(1)}, bf16[2,1024,768]{2,1,0:T(8,128)(2,1)}, u32[]{:S(2)}) copy-start(bf16[2,1024,768]{2,1,0:T(8,128)(2,1)} %param.14) | copy-start | bytes 9437188
  96.7 295.8 %all-gather.14.cloned.1.call-start = ((), (), s32[]{:S(2)}) async-start(), calls=%async_computation.15 | async-start | bytes 3538944 | tf_op jit(solution)/shard_map/all_gather | solution.py:60
  166.4 289.5 %all-gather.8.cloned.1.call-start = ((), (), s32[]{:S(2)}) async-start(), calls=%async_computation.8 | async-start | bytes 3538944 | tf_op jit(solution)/shard_map/all_gather | solution.py:60
  331.4 187.9 %all-gather.12.cloned.1.call-start = ((), (), s32[]{:S(2)}) async-start(), calls=%async_computation.12 | async-start | bytes 3538944 | tf_op jit(solution)/shard_map/all_gather | solution.py:60
  332.2 255.1 %reduce-scatter.17.cloned.1.call-start = ((), (), s32[]{:S(2)}) async-start(), calls=%async_computation.16 | async-start | bytes 2506752 | tf_op jit(solution)/shard_map/reduce_scatter | solution.py:64
  399.5 119.7 %copy-start.4 = (bf16[2,768,1024]{2,1,0:T(8,128)(2,1)S(1)}, bf16[2,768,1024]{2,1,0:T(8,128)(2,1)}, u32[]{:S(2)}) copy-start(bf16[2,768,1024]{2,1,0:T(8,128)(2,1)} %param.11) | copy-start | bytes 9437188
  399.6 254.0 %reduce-scatter.9.cloned.1.call-start = ((), (), s32[]{:S(2)}) async-start(), calls=%async_computation.9 | async-start | bytes 2506752 | tf_op jit(solution)/shard_map/reduce_scatter | solution.py:64
  462.8 257.2 %reduce-scatter.13.cloned.1.call-start = ((), (), s32[]{:S(2)}) async-start(), calls=%async_computation.13 | async-start | bytes 2506752 | tf_op jit(solution)/shard_map/reduce_scatter | solution.py:64
  525.2 7.1 copy-start.5
  525.2 7.1 copy-start.6
Sparse Core Ops, SparseCore 0:
  10.2 36.5 all-gather.5
  49.1 34.4 all-gather.9
  87.4 77.0 reduce-scatter.14
  168.7 77.9 reduce-scatter.10
  251.0 78.0 reduce-scatter.6
  331.2 61.2 all-gather.13
  395.4 60.4 all-gather.7
  458.8 60.4 all-gather.11
  521.7 65.5 reduce-scatter.16
  589.6 63.9 reduce-scatter.8
  656.0 63.9 reduce-scatter.12
where the time goes:
time: 729 us; the launch traced here: 728 us
  waiting for transfers between devices  647 us (89%)
  matrix products  58.7 us (8%)
  between operations  14 us (2%)
    reduce_scatter x3, waiting for transfers between devices, edata_sum(): lax.psum_scatter(term_fn(jnp.int32(0), share_rows * lax.axis_size('edata'...  230 us
    reduce_scatter x3, waiting for transfers between devices, tensor_sum(): lax.psum_scatter(term_fn(jnp.int32(0), owner_rows * lax.axis_size('tensor...  180 us
    all_gather x3, waiting for transfers between devices, edata_sum(): acted = lax.all_gather(act_fn(summed), 'edata', axis=0, tiled=True)  173 us
    all_gather x1, waiting for transfers between devices, shards(): lax.all_gather(picked, 'tensor', axis=0, tiled=True)  34.4 us
    all_gather x1, waiting for transfers between devices, shards(): lax.all_gather(scaled, 'tensor', axis=0, tiled=True)  28.7 us
  transfers between devices with their start and end apart: 11, of which 11 were waited for; matrix products, arithmetic and copies ran while one was open for 8% of the time, Pallas kernels for 0%

commit v1 on v0

--- a/solution.py
+++ b/solution.py
@@ -43,7 +43,9 @@
         "cet,td->ced", combine, cotangent.astype(jnp.float32), precision=lax.Precision.HIGHEST
     ).astype(jnp.bfloat16)
     gathered_x, gathered_g = (
-        lax.all_gather(picked, "tensor", axis=0, tiled=True),
+        jnp.concatenate(
+            lax.all_to_all(jnp.stack([picked] * lax.axis_size("tensor")), "tensor", 0, 0), axis=0
+        ),
         lax.all_gather(scaled, "tensor", axis=0, tiled=True),
     )
     routed = gathered_x.shape[0]

time: 729 us -> 681 us (0.934)
  waiting for transfers between devices: 647 us -> 544 us
  blocking collectives: 0 us -> 44.8 us
  local copies, waits for them, and re-layouts: 2.07 us -> 10.9 us
    reduce_scatter x3 -> x2, waiting for transfers between devices: 180 us -> 129 us  [tensor_sum(): lax.psum_scatter(term_fn(jnp.int32(0), owner_rows * lax.axis_size('tensor...]
    all_to_all x0 -> x1, blocking collectives: none -> 44.8 us  [shards(): lax.all_to_all(jnp.stack([picked] * lax.axis_size('tensor')), 'tensor', 0...]
    all_gather x1 -> x0, waiting for transfers between devices: 34.4 us -> none  [shards(): lax.all_gather(picked, 'tensor', axis=0, tiled=True)]
    all_gather x1, waiting for transfers between devices: 28.7 us -> 0.02 us  [shards(): lax.all_gather(scaled, 'tensor', axis=0, tiled=True)]
    unnamed x11, waiting for transfers between devices: 0.86 us -> 25.2 us
    all_gather x3, waiting for transfers between devices: 173 us -> 164 us  [edata_sum(): acted = lax.all_gather(act_fn(summed), 'edata', axis=0, tiled=True)]
  transfers between devices with their start and end apart: 11 -> 10, of which waited for: 11 -> 9; matrix products, arithmetic and copies ran while one was open for 8% -> 10% of each run, Pallas kernels for 0% -> 0%
where the time goes in v1:
time: 681 us
  waiting for transfers between devices  544 us (80%)
  matrix products  57.5 us (8%)
  blocking collectives  44.8 us (7%)
  between operations  16.1 us (2%)
  local copies, waits for them, and re-layouts  10.9 us (2%)
    reduce_scatter x3, waiting for transfers between devices, edata_sum(): lax.psum_scatter(term_fn(jnp.int32(0), share_rows * lax.axis_size('edata'...  226 us
    all_gather x3, waiting for transfers between devices, edata_sum(): acted = lax.all_gather(act_fn(summed), 'edata', axis=0, tiled=True)  164 us
    reduce_scatter x2, waiting for transfers between devices, tensor_sum(): lax.psum_scatter(term_fn(jnp.int32(0), owner_rows * lax.axis_size('tensor...  129 us
    all_to_all x1, blocking collectives, shards(): lax.all_to_all(jnp.stack([picked] * lax.axis_size('tensor')), 'tensor', 0...  44.8 us
    unnamed x11, waiting for transfers between devices  25.2 us
    dot_general x2, matrix products, partial_down(): jnp.einsum('ref,efd->red', source, weight, preferred_element_type=jnp.flo...  15.5 us
  transfers between devices with their start and end apart: 10, of which 9 were waited for; matrix products, arithmetic and copies ran while one was open for 10% of the time, Pallas kernels for 0%

profile of v1, /device:TPU:4, one launch (start us, length us, event | category | flops | bytes accessed | tf_op | source)
XLA Modules:
  0.0 680.6 jit_solution(2000074693101633587)
XLA Ops:
  12.8 44.8 %all_to_all.5 = bf16[16,48,2,768]{3,1,2,0:T(8,128)(2,1)S(1)} all-to-all(bf16[16,48,2,768]{3,1,2,0:T(8,128)(2,1)S(1)} %stack.8), channel_id=1, replica_groups=mesh['edata'=8,'tensor'=16] {'tensor'}, dimensions={0} | all-to-all | bytes 4718592 | tf_op jit(solution)/shard_map/all_to_all | solution.py:47
  57.8 1.8 copy-done.1
  59.5 4.1 convert_bitcast_fusion
  63.7 5.8 convert_bitcast_fusion.2
  69.7 6.9 %convert_bitcast_fusion.1 = bf16[768,2,1024]{2,0,1:T(8,128)(2,1)} fusion(bf16[768,2,768]{2,0,1:T(8,128)(2,1)} %all-gather.7.cloned.1.call-done, bf16[2,1024,768]{2,1,0:T(8,128)(2,1)} %param.12), kind=kOutput, calls=%fused_computation.9 | convolution fusion | flops 2417491968 | bytes 8650752 | tf_op jit(solution)/shard_map/red,efd->ref/dot_general | solution.py:88
  76.7 63.3 %reduce-scatter.14.cloned.1.call-done = bf16[96,2,1024]{2,0,1:T(8,128)(2,1)} async-done(((bf16[768,2,1024]{2,0,1:T(8,128)(2,1)}), bf16[96,2,1024]{2,0,1:T(8,128)(2,1)}) %reduce-scatter.14.cloned.1.call-update) | async-done | bytes 393232 | tf_op jit(solution)/shard_map/reduce_scatter | solution.py:56
  140.0 2.0 fusion.12
  142.0 80.3 %reduce-scatter.6.cloned.1.call-done = bf16[96,2,1024]{2,0,1:T(8,128)(2,1)} async-done(((bf16[768,2,1024]{2,0,1:T(8,128)(2,1)}), bf16[96,2,1024]{2,0,1:T(8,128)(2,1)}) %reduce-scatter.6.cloned.1.call-update) | async-done | bytes 393232 | tf_op jit(solution)/shard_map/reduce_scatter | solution.py:56
  222.4 82.4 %reduce-scatter.10.cloned.1.call-done = bf16[96,2,1024]{2,0,1:T(8,128)(2,1)} async-done(((bf16[768,2,1024]{2,0,1:T(8,128)(2,1)}), bf16[96,2,1024]{2,0,1:T(8,128)(2,1)}) %reduce-scatter.10.cloned.1.call-update) | async-done | bytes 393232 | tf_op jit(solution)/shard_map/reduce_scatter | solution.py:56
  304.8 2.4 fusion.19
  308.0 60.1 %all-gather.11.cloned.1.call-done = bf16[768,2,1024]{2,0,1:T(8,128)(2,1)} async-done(((bf16[96,2,1024]{2,0,1:T(8,128)(2,1)}), bf16[768,2,1024]{2,0,1:T(8,128)(2,1)}) %all-gather.11.cloned.1.call-update) | async-done | bytes 3145744 | tf_op jit(solution)/shard_map/all_gather | solution.py:62
  368.1 8.7 %convert_bitcast_fusion.3 = bf16[768,2,768]{0,2,1:T(8,128)(2,1)} fusion(bf16[768,2,1024]{2,0,1:T(8,128)(2,1)} %all-gather.11.cloned.1.call-done, bf16[2,1024,768]{2,1,0:T(8,128)(2,1)} %param.12, bf16[2,1024,768]{2,1,0:T(8,128)(2,1)} %param.14), kind=kOutput, calls=%fused_computation.11 | convolution fusion | flops 2426535936 | bytes 11796480 | tf_op jit(solution)/shard_map/ref,efd->red/dot_general | solution.py:83
  376.7 6.9 %copy.38 = bf16[768,2,768]{2,1,0:T(2,128)(2,1)} copy(bf16[768,2,768]{0,2,1:T(8,128)(2,1)} %convert_bitcast_fusion.3) | data formatting | bytes 4718592 | tf_op jit(solution)/shard_map/convert_element_type | solution.py:67
  383.9 46.7 %all-gather.5.cloned.1.call-done = bf16[768,2,1024]{2,0,1:T(8,128)(2,1)} async-done(((bf16[96,2,1024]{2,0,1:T(8,128)(2,1)}), bf16[768,2,1024]{2,0,1:T(8,128)(2,1)}) %all-gather.5.cloned.1.call-update) | async-done | bytes 3145744 | tf_op jit(solution)/shard_map/all_gather | solution.py:62
  430.6 6.8 %convert_bitcast_fusion.5 = bf16[768,2,768]{2,0,1:T(8,128)(2,1)} fusion(bf16[768,2,1024]{2,0,1:T(8,128)(2,1)} %all-gather.5.cloned.1.call-done, bf16[2,1024,768]{2,1,0:T(8,128)(2,1)} %param.12), kind=kOutput, calls=%fused_computation.13 | convolution fusion | flops 2417098752 | bytes 8650752 | tf_op jit(solution)/shard_map/ref,efd->red/dot_general | solution.py:83
  437.6 56.8 %all-gather.9.cloned.1.call-done = bf16[768,2,1024]{2,0,1:T(8,128)(2,1)} async-done(((bf16[96,2,1024]{2,0,1:T(8,128)(2,1)}), bf16[768,2,1024]{2,0,1:T(8,128)(2,1)}) %all-gather.9.cloned.1.call-update) | async-done | bytes 3145744 | tf_op jit(solution)/shard_map/all_gather | solution.py:62
  494.4 6.9 %convert_bitcast_fusion.4 = bf16[768,2,768]{2,0,1:T(8,128)(2,1)} fusion(bf16[768,2,1024]{2,0,1:T(8,128)(2,1)} %all-gather.9.cloned.1.call-done, bf16[2,768,1024]{2,1,0:T(8,128)(2,1)} %param.11), kind=kOutput, calls=%fused_computation.12 | convolution fusion | flops 2417098752 | bytes 8650752 | tf_op jit(solution)/shard_map/ref,edf->red/dot_general | solution.py:115
  502.6 7.1 %convolution_convert_fusion = bf16[2,1024,768]{2,1,0:T(8,128)(2,1)} fusion(bf16[768,2,1024]{2,0,1:T(8,128)(2,1)} %all-gather.5.cloned.1.call-done, bf16[768,2,768]{2,0,1:T(8,128)(2,1)} %all-gather.7.cloned.1.call-done), kind=kOutput, calls=%fused_computation.14 | convolution fusion | flops 2417491968 | bytes 8650752 | tf_op jit(solution)/shard_map/ref,red->efd/dot_general | solution.py:101
  509.7 4.1 convolution_convert_fusion.1
  513.7 24.4 %all-reduce.3.cloned.1.call-done = bf16[768,2,768]{2,1,0:T(2,128)(2,1)} async-done(((bf16[768,2,768]{2,1,0:T(2,128)(2,1)}), bf16[768,2,768]{2,1,0:T(2,128)(2,1)}) %all-reduce.3.cloned.1.call-update) | async-done | bytes 2359312
  540.2 65.0 %reduce-scatter.8.cloned.1.call-done = bf16[48,2,768]{2,0,1:T(8,128)(2,1)} async-done(((bf16[768,2,768]{2,0,1:T(8,128)(2,1)}), bf16[48,2,768]{2,0,1:T(8,128)(2,1)}) %reduce-scatter.8.cloned.1.call-update) | async-done | bytes 147472 | tf_op jit(solution)/shard_map/reduce_scatter | solution.py:66
  605.2 2.0 fusion.6
  607.2 64.3 %reduce-scatter.12.cloned.1.call-done = bf16[48,2,768]{2,0,1:T(8,128)(2,1)} async-done(((bf16[768,2,768]{2,0,1:T(8,128)(2,1)}), bf16[48,2,768]{2,0,1:T(8,128)(2,1)}) %reduce-scatter.12.cloned.1.call-update) | async-done | bytes 147472 | tf_op jit(solution)/shard_map/reduce_scatter | solution.py:66
  671.5 2.0 fusion.7
  (49 shorter events, 8.8 us)
Async XLA Ops:
  8.0 2.3 copy-start
  8.0 61.7 %all-gather.7.cloned.1.call-start = ((), (), s32[]{:S(2)}) async-start(), calls=%async_computation.9 | async-start | bytes 2506752 | tf_op jit(solution)/shard_map/all_gather | solution.py:49
  11.3 128.7 %reduce-scatter.14.cloned.1.call-start = ((), (), s32[]{:S(2)}) async-start(), calls=%async_computation.13 | async-start | bytes 3538944 | tf_op jit(solution)/shard_map/reduce_scatter | solution.py:56
  12.7 45.0 %copy-start.2 = (bf16[2,768,1024]{2,1,0:T(8,128)(2,1)S(1)}, bf16[2,768,1024]{2,1,0:T(8,128)(2,1)}, u32[]{:S(2)}) copy-start(bf16[2,768,1024]{2,1,0:T(8,128)(2,1)} %param.11) | copy-start | bytes 9437188
  57.6 1.9 copy-start.1
  63.7 158.7 %reduce-scatter.6.cloned.1.call-start = ((), (), s32[]{:S(2)}) async-start(), calls=%async_computation.6 | async-start | bytes 3538944 | tf_op jit(solution)/shard_map/reduce_scatter | solution.py:56
  69.6 235.2 %reduce-scatter.10.cloned.1.call-start = ((), (), s32[]{:S(2)}) async-start(), calls=%async_computation.10 | async-start | bytes 3538944 | tf_op jit(solution)/shard_map/reduce_scatter | solution.py:56
  76.6 291.4 %all-gather.11.cloned.1.call-start = ((), (), s32[]{:S(2)}) async-start(), calls=%async_computation.14 | async-start | bytes 3538944 | tf_op jit(solution)/shard_map/all_gather | solution.py:62
  142.0 288.7 %all-gather.5.cloned.1.call-start = ((), (), s32[]{:S(2)}) async-start(), calls=%async_computation.7 | async-start | bytes 3538944 | tf_op jit(solution)/shard_map/all_gather | solution.py:62
  307.2 187.2 %all-gather.9.cloned.1.call-start = ((), (), s32[]{:S(2)}) async-start(), calls=%async_computation.11 | async-start | bytes 3538944 | tf_op jit(solution)/shard_map/all_gather | solution.py:62
  307.9 230.2 %all-reduce.3.cloned.1.call-start = ((), (), s32[]{:S(2)}) async-start(), calls=%async_computation.15 | async-start | bytes 4718592
  383.7 221.5 %reduce-scatter.8.cloned.1.call-start = ((), (), s32[]{:S(2)}) async-start(), calls=%async_computation.8 | async-start | bytes 2506752 | tf_op jit(solution)/shard_map/reduce_scatter | solution.py:66
  437.5 63.8 %copy-start.4 = (u32[128]{0:T(128)S(1)}, u32[128]{0:T(128)}, u32[]{:S(2)}) copy-start(u32[128]{0:T(128)} %constant.29) | copy-start | bytes 1540
  437.5 234.0 %reduce-scatter.12.cloned.1.call-start = ((), (), s32[]{:S(2)}) async-start(), calls=%async_computation.12 | async-start | bytes 2506752 | tf_op jit(solution)/shard_map/reduce_scatter | solution.py:66
  502.5 7.1 %copy-start.3 = (bf16[768,2,1024]{2,0,1:T(8,128)(2,1)S(1)}, bf16[768,2,1024]{2,0,1:T(8,128)(2,1)}, u32[]{:S(2)}) copy-start(bf16[768,2,1024]{2,0,1:T(8,128)(2,1)} %all-gather.9.cloned.1.call-done) | copy-start | bytes 9437188
Sparse Core Ops, SparseCore 0:
  11.4 52.9 all-gather.6
  383.8 154.2 all-reduce.2
  540.6 64.6 reduce-scatter.7
  607.5 63.9 reduce-scatter.11
Sparse Core Ops, SparseCore 1:
  63.8 76.2 reduce-scatter.13
  144.3 78.1 reduce-scatter.5
  226.7 78.1 reduce-scatter.9
  307.2 60.8 all-gather.10
  370.4 60.2 all-gather.4
  433.6 60.8 all-gather.8
